TPU v7x, 32 devices: a whole 2x2x4 slice. The times are simulated.
32 devices in a mesh: rep: 4 (over z), shard: 8 (over y, x, core).
Axes of the slice: x: 2, y: 2, z: 4, core: 2. Of those that a mesh axis runs over, the one named last changes fastest.
Arguments:
- tokens: bfloat16 [8192, 2048], P(('rep', 'shard')), may hold values from -6 to 6
- cotangent: bfloat16 [8192, 2048], P(('rep', 'shard')), may hold values from -6 to 6
- placement_order: int32 [4, 8, 2, 128], P('rep', 'shard'), may hold values from 0 to 127, each once within a row
- seq_lengths: int32 [4, 2, 8], P('rep'), may hold values from 0 to 1024, as said below
- ln_gain: bfloat16 [2048], P('shard'), may hold values from 0.25 to 1.75
- ln_bias: bfloat16 [2048], P('shard'), may hold values from -4 to 4
- qkv_weight: bfloat16 [2048, 6144], P('shard'), may hold values from -0.125 to 0.125
- qkv_bias: bfloat16 [6144], P('shard'), may hold values from -6 to 6
- dense_weight: bfloat16 [2048, 2048], P('shard'), may hold values from -2 to 2
- dense_bias: bfloat16 [2048], P('shard'), may hold values from -4 to 4
- fc1_weight: bfloat16 [2048, 8192], P('shard'), may hold values from -0.125 to 0.125
- fc1_bias: bfloat16 [8192], P('shard'), may hold values from -4 to 4
- fc2_weight: bfloat16 [8192, 2048], P('shard'), may hold values from -0.0625 to 0.0625
- fc2_bias: bfloat16 [2048], P('shard'), may hold values from -4 to 4
Outputs:
- mixed: bfloat16 [8192, 2048], P(('rep', 'shard'))
- token_grad: bfloat16 [8192, 2048], P(('rep', 'shard'))
- grad_ln_gain: float32 [2048], P('shard')
- grad_ln_bias: float32 [2048], P('shard')
- grad_qkv_weight: float32 [2048, 6144], P('shard')
- grad_qkv_bias: float32 [6144], P('shard')
- grad_dense_weight: float32 [2048, 2048], P('shard')
- grad_dense_bias: float32 [2048], P('shard')
- grad_fc1_weight: float32 [2048, 8192], P('shard')
- grad_fc1_bias: float32 [8192], P('shard')
- grad_fc2_weight: float32 [8192, 2048], P('shard')
- grad_fc2_bias: float32 [2048], P('shard')
Inputs may be any that keep to these rules, and one draw needn't show every extreme that they name: `seq_lengths`: for replica group r and micro-batch m, entry j is the length of the sequence that starts at block j, or 0 where block j continues the sequence before it. Entry 0 is positive. A sequence that starts at block j runs to the block before the next positive entry (or to the last block), b blocks, and its length is over 128 * (b - 1) and at most 128 * b; b is at most 8; some sequence has 1024 tokens. `placement_order`: each device's row for a micro-batch is a permutation; a value b sends that row to the device of shard index b // 16 of the same replica group.
All inputs are finite; a program needn't handle non-finite values.
Results may differ from a plain program's by a relative error of at most 0.013.
Values may be sent and summed in bfloat16 or wider, within the bound.
A program may use at most 704 MiB of HBM per device.

v0:
```python
import math
import jax
import jax.numpy as jnp
from jax import lax
from jax.sharding import PartitionSpec as P

HEADS = 32
HDIM = 64
ROT = 32
BLOCK = 128
MICRO = 2
MAXBLK = 8


def shifted(block, axis, distance):
    devices = range(lax.axis_size(axis))
    route = [(i - distance, i) for i in devices if i - distance in devices]
    return lax.ppermute(block, axis, route)


def contract_last(left, right):
    return lax.dot_general(
        left, right, (((1,), (1,)), ((), ())), preferred_element_type=jnp.float32
    )


def contract_first(left, right):
    return lax.dot_general(
        left, right, (((0,), (0,)), ((), ())), preferred_element_type=jnp.float32
    )


def normalize(inputs, gain_vec, bias_vec):
    average = jnp.mean(inputs, axis=-1, keepdims=True)
    centered = inputs - average
    variance = jnp.mean(centered * centered, axis=-1, keepdims=True)
    return centered * lax.rsqrt(variance + 1e-05) * gain_vec + bias_vec


def rotary_tables(position):
    half_dim = ROT // 2
    freqs = jnp.exp(-math.log(10000.0) * jnp.arange(half_dim, dtype=jnp.float32) * 2.0 / ROT)
    angles = position.astype(jnp.float32)[:, None] * freqs[None, :]
    angles = jnp.concatenate([angles, angles], axis=1)
    return (jnp.cos(angles)[:, None, :], jnp.sin(angles)[:, None, :])


def rotate(heads, cosine_table, sine_table):
    half_dim = ROT // 2
    turned_part = heads[..., :ROT]
    swapped = jnp.concatenate([-turned_part[..., half_dim:], turned_part[..., :half_dim]], axis=-1)
    return jnp.concatenate(
        [turned_part * cosine_table + swapped * sine_table, heads[..., ROT:]], axis=-1
    )


def gelu_tanh(values):
    return jax.nn.gelu(values, approximate=True)


def block_meta(lengths_row, first_row, span_rows):
    block_count = lengths_row.shape[0]
    blocks = jnp.arange(block_count, dtype=jnp.int32)
    begins = jnp.max(
        jnp.where(
            (lengths_row[None, :] > 0) & (blocks[None, :] <= blocks[:, None]), blocks[None, :], 0
        ),
        axis=1,
    )
    begin_length = jnp.sum(
        jnp.where(begins[:, None] == blocks[None, :], lengths_row[None, :], 0), axis=1
    )
    global_rows = first_row + jnp.arange(span_rows, dtype=jnp.int32)
    picks = (global_rows // BLOCK)[:, None] == blocks[None, :]
    segment = jnp.sum(jnp.where(picks, begins[None, :], 0), axis=1)
    limit = jnp.sum(jnp.where(picks, begin_length[None, :], 0), axis=1)
    position = global_rows - segment * BLOCK
    usable = (global_rows >= 0) & (position < limit)
    return (segment, position, usable)


def reduce_grads(hn_rows, dqkv_rows, dup_rows, ob_rows, gact_rows, gy_rows, vectors):
    wide = lax.psum_scatter(
        jnp.concatenate(
            [
                contract_first(hn_rows, dqkv_rows),
                contract_first(hn_rows, dup_rows),
                contract_first(ob_rows, gy_rows),
            ],
            axis=1,
        ).astype(jnp.bfloat16),
        "shard",
        scatter_dimension=0,
        tiled=True,
    ).astype(jnp.float32)
    deep = lax.psum_scatter(
        contract_first(gact_rows, gy_rows).astype(jnp.bfloat16),
        "shard",
        scatter_dimension=0,
        tiled=True,
    ).astype(jnp.float32)
    scattered = (
        lax.psum_scatter(
            vectors[0].astype(jnp.bfloat16), "shard", scatter_dimension=0, tiled=True
        ).astype(jnp.float32),
        lax.psum_scatter(
            vectors[1].astype(jnp.bfloat16), "shard", scatter_dimension=0, tiled=True
        ).astype(jnp.float32),
        lax.psum_scatter(
            vectors[2].astype(jnp.bfloat16), "shard", scatter_dimension=0, tiled=True
        ).astype(jnp.float32),
        lax.psum_scatter(
            vectors[3].astype(jnp.bfloat16), "shard", scatter_dimension=0, tiled=True
        ).astype(jnp.float32),
        lax.psum_scatter(
            vectors[4].astype(jnp.bfloat16), "shard", scatter_dimension=0, tiled=True
        ).astype(jnp.float32),
    )
    return lax.psum(
        (wide, deep, scattered[0], scattered[1], scattered[2], scattered[3], scattered[4]), "rep"
    )


def body(
    tokens,
    cotangent,
    placement_order,
    seq_lengths,
    ln_gain,
    ln_bias,
    qkv_weight,
    qkv_bias,
    dense_weight,
    dense_bias,
    fc1_weight,
    fc1_bias,
    fc2_weight,
    fc2_bias,
):
    group_size = lax.axis_size("shard")
    shard_pos = lax.axis_index("shard")
    model_width = tokens.shape[1]
    ff_width = fc1_weight.shape[1]
    row_count = tokens.shape[0] // MICRO
    cap_rows = row_count // group_size
    blk_dev = row_count // BLOCK
    reach = (MAXBLK - 1 + blk_dev - 1) // blk_dev
    span_rows = (reach + 1) * row_count
    scale = 1.0 / math.sqrt(HDIM)
    orders = placement_order[0, 0]
    micro_ids = jnp.arange(MICRO, dtype=jnp.int32)[:, None]
    spots = jnp.broadcast_to(jnp.arange(row_count, dtype=jnp.int32)[None, :], orders.shape)
    inverse = jnp.zeros_like(orders).at[micro_ids, orders].set(spots)

    def to_buffer(array):
        return jnp.take_along_axis(
            array.reshape(MICRO, row_count, model_width), inverse[:, :, None], axis=1
        ).reshape(MICRO, group_size, cap_rows, model_width)

    arrived = (
        lax.all_to_all(to_buffer(tokens), "shard", split_axis=1, concat_axis=1, tiled=True),
        lax.all_to_all(to_buffer(cotangent), "shard", split_axis=1, concat_axis=1, tiled=True),
    )
    att_x = arrived[0].reshape(MICRO, row_count, model_width)
    att_g = arrived[1].reshape(MICRO, row_count, model_width)
    shards = (
        ln_gain,
        ln_bias,
        qkv_weight,
        qkv_bias,
        dense_weight,
        dense_bias,
        fc1_weight,
        fc1_bias,
        fc2_weight,
        fc2_bias,
    )
    gathered_once = (
        lax.all_gather(shards[0], "shard", axis=0, tiled=True),
        lax.all_gather(shards[1], "shard", axis=0, tiled=True),
        lax.all_gather(shards[2], "shard", axis=0, tiled=True),
        lax.all_gather(shards[3], "shard", axis=0, tiled=True),
        lax.all_gather(shards[4], "shard", axis=0, tiled=True),
        lax.all_gather(shards[5], "shard", axis=0, tiled=True),
        lax.all_gather(shards[6], "shard", axis=0, tiled=True),
        lax.all_gather(shards[7], "shard", axis=0, tiled=True),
        lax.all_gather(shards[8], "shard", axis=0, tiled=True),
        lax.all_gather(shards[9], "shard", axis=0, tiled=True),
    )
    mixed_list = []
    grad_list = []
    stored = []
    totals = None
    for micro_idx in range(MICRO):
        gain_full, lnb_full, w_qkv, b_qkv, w_dense, b_dense, w_fc1, b_fc1, w_fc2, b_fc2 = (
            gathered_once
        )
        segment, position, usable = block_meta(
            seq_lengths[0, micro_idx], (shard_pos - reach) * row_count, span_rows
        )
        seg_query = segment[reach * row_count :]
        pos_query = position[reach * row_count :]
        valid_query = usable[reach * row_count :]
        inputs = att_x[micro_idx].astype(jnp.float32)
        normed, norm_pull = jax.vjp(
            normalize, inputs, gain_full.astype(jnp.float32), lnb_full.astype(jnp.float32)
        )
        hn_rows = normed.astype(jnp.bfloat16)
        qkv = jnp.dot(hn_rows, w_qkv, preferred_element_type=jnp.float32) + b_qkv.astype(
            jnp.float32
        )
        queries = qkv[:, :model_width].reshape(row_count, HEADS, HDIM)
        keys_raw = qkv[:, model_width : 2 * model_width].reshape(row_count, HEADS, HDIM)
        value_rows = qkv[:, 2 * model_width :].astype(jnp.bfloat16)
        cosine_table, sine_table = rotary_tables(pos_query)
        turned, turn_pull = jax.vjp(
            lambda first, second: (
                rotate(first, cosine_table, sine_table),
                rotate(second, cosine_table, sine_table),
            ),
            queries,
            keys_raw,
        )
        q_low = turned[0].astype(jnp.bfloat16)
        key_rows = turned[1].astype(jnp.bfloat16).reshape(row_count, model_width)
        older = []
        for shift_by in range(1, reach + 1):
            older.append(shifted((key_rows, value_rows), "shard", shift_by))
        key_win = jnp.concatenate(
            [received[0] for received in reversed(older)] + [key_rows], axis=0
        ).reshape(span_rows, HEADS, HDIM)
        val_win = jnp.concatenate(
            [received[1] for received in reversed(older)] + [value_rows], axis=0
        ).reshape(span_rows, HEADS, HDIM)
        allowed = (
            (seg_query[:, None] == segment[None, :])
            & (position[None, :] <= pos_query[:, None])
            & usable[None, :]
        )
        scores = (
            jnp.einsum("qhd,khd->hqk", q_low, key_win, preferred_element_type=jnp.float32) * scale
        )
        masked = jnp.where(allowed[None], scores, -1e30)
        top_score = jnp.max(masked, axis=-1, keepdims=True)
        expo = jnp.exp(masked - top_score)
        denom = jnp.sum(expo, axis=-1, keepdims=True)
        log_total = top_score + jnp.log(denom)
        probs = expo / denom
        attn_rows = jnp.einsum(
            "hqk,khd->qhd", probs.astype(jnp.bfloat16), val_win, preferred_element_type=jnp.float32
        )
        ob_rows = attn_rows.reshape(row_count, model_width).astype(jnp.bfloat16)
        attn_proj = jnp.dot(ob_rows, w_dense, preferred_element_type=jnp.float32) + b_dense.astype(
            jnp.float32
        )
        upper = jnp.dot(hn_rows, w_fc1, preferred_element_type=jnp.float32) + b_fc1.astype(
            jnp.float32
        )
        activated, gelu_pull = jax.vjp(gelu_tanh, upper)
        gact_rows = activated.astype(jnp.bfloat16)
        mlp_out = jnp.dot(gact_rows, w_fc2, preferred_element_type=jnp.float32) + b_fc2.astype(
            jnp.float32
        )
        mixed_rows = inputs + jnp.where(valid_query[:, None], attn_proj + mlp_out, 0.0)
        mixed_list.append(mixed_rows.astype(jnp.bfloat16))
        gy_rows = jnp.where(valid_query[:, None], att_g[micro_idx], jnp.zeros((), jnp.bfloat16))
        d_act = contract_last(gy_rows, w_fc2)
        dup_rows = gelu_pull(d_act)[0].astype(jnp.bfloat16)
        d_out = contract_last(gy_rows, w_dense).astype(jnp.bfloat16).reshape(row_count, HEADS, HDIM)
        again = (
            jnp.einsum("qhd,khd->hqk", q_low, key_win, preferred_element_type=jnp.float32) * scale
        )
        probs_again = jnp.where(allowed[None], jnp.exp(again - log_total), 0.0)
        d_probs = jnp.einsum("qhd,khd->hqk", d_out, val_win, preferred_element_type=jnp.float32)
        row_delta = jnp.sum(probs_again * d_probs, axis=-1, keepdims=True)
        d_scores = (probs_again * (d_probs - row_delta)).astype(jnp.bfloat16)
        d_query = (
            jnp.einsum("hqk,khd->qhd", d_scores, key_win, preferred_element_type=jnp.float32)
            * scale
        )
        d_keywin = (
            jnp.einsum("hqk,qhd->khd", d_scores, q_low, preferred_element_type=jnp.float32) * scale
        ).reshape(span_rows, model_width)
        d_valwin = jnp.einsum(
            "hqk,qhd->khd",
            probs_again.astype(jnp.bfloat16),
            d_out,
            preferred_element_type=jnp.float32,
        ).reshape(span_rows, model_width)
        key_total = d_keywin[reach * row_count :]
        value_total = d_valwin[reach * row_count :]
        for shift_by in range(1, reach + 1):
            lower_row = (reach - shift_by) * row_count
            returned = (
                shifted(
                    d_keywin[lower_row : lower_row + row_count].astype(jnp.bfloat16),
                    "shard",
                    -shift_by,
                ).astype(jnp.float32),
                shifted(
                    d_valwin[lower_row : lower_row + row_count].astype(jnp.bfloat16),
                    "shard",
                    -shift_by,
                ).astype(jnp.float32),
            )
            key_total = key_total + returned[0]
            value_total = value_total + returned[1]
        unturned = turn_pull((d_query, key_total.reshape(row_count, HEADS, HDIM)))
        dqkv_rows = jnp.concatenate(
            [
                unturned[0].reshape(row_count, model_width),
                unturned[1].reshape(row_count, model_width),
                value_total,
            ],
            axis=1,
        ).astype(jnp.bfloat16)
        d_normed = contract_last(dqkv_rows, w_qkv) + contract_last(dup_rows, w_fc1)
        d_inputs, d_gain, d_lnbias = norm_pull(d_normed)
        grad_list.append((att_g[micro_idx].astype(jnp.float32) + d_inputs).astype(jnp.bfloat16))
        vectors = (
            jnp.sum(dqkv_rows.astype(jnp.float32), axis=0),
            jnp.sum(dup_rows.astype(jnp.float32), axis=0),
            jnp.sum(gy_rows.astype(jnp.float32), axis=0),
            d_gain,
            d_lnbias,
        )
        stored.append((hn_rows, dqkv_rows, dup_rows, ob_rows, gact_rows, gy_rows, vectors))
    joined = [jnp.concatenate([entry[slot] for entry in stored], axis=0) for slot in range(6)]
    vector_sums = tuple(
        (jnp.sum(jnp.stack([entry[6][slot] for entry in stored]), axis=0) for slot in range(5))
    )
    totals = reduce_grads(
        joined[0], joined[1], joined[2], joined[3], joined[4], joined[5], vector_sums
    )
    mixed_back = jnp.stack(mixed_list).reshape(MICRO, group_size, cap_rows, model_width)
    grads_back = jnp.stack(grad_list).reshape(MICRO, group_size, cap_rows, model_width)
    homeward = (
        lax.all_to_all(mixed_back, "shard", split_axis=1, concat_axis=1, tiled=True),
        lax.all_to_all(grads_back, "shard", split_axis=1, concat_axis=1, tiled=True),
    )

    def from_buffer(array):
        return jnp.take_along_axis(
            array.reshape(MICRO, row_count, model_width), orders[:, :, None], axis=1
        ).reshape(MICRO * row_count, model_width)

    wide, deep, bias_qkv, bias_fc1, bias_out, gain_grad, lnbias_grad = totals
    qkv_cols = 3 * model_width
    return (
        from_buffer(homeward[0]),
        from_buffer(homeward[1]),
        gain_grad,
        lnbias_grad,
        wide[:, :qkv_cols],
        bias_qkv,
        wide[:, qkv_cols + ff_width :],
        bias_out,
        wide[:, qkv_cols : qkv_cols + ff_width],
        bias_fc1,
        deep,
        bias_out,
    )


def solution(mesh):
    placed = (
        P(("rep", "shard"), None),
        P(("rep", "shard"), None),
        P("rep", "shard", None, None),
        P("rep", None, None),
        P("shard"),
        P("shard"),
        P("shard", None),
        P("shard"),
        P("shard", None),
        P("shard"),
        P("shard", None),
        P("shard"),
        P("shard", None),
        P("shard"),
    )
    return jax.shard_map(
        body,
        mesh=mesh,
        in_specs=placed,
        out_specs=(
            P(("rep", "shard"), None),
            P(("rep", "shard"), None),
            P("shard"),
            P("shard"),
            P("shard", None),
            P("shard"),
            P("shard", None),
            P("shard"),
            P("shard", None),
            P("shard"),
            P("shard", None),
            P("shard"),
        ),
        check_vma=False,
    )
```

profile of v0, /device:TPU:0, one launch (start us, length us, event | category | flops | bytes accessed | tf_op | source)
XLA Modules:
  0.0 2567.9 jit_solution(3848046647579262749)
XLA Ops:
  10.6 11.4 scatter_fusion
  39.3 24.7 all-gather.1
  64.0 9.3 all-gather
  73.4 7.7 all_gather.37
  81.1 9.2 all-gather.2
  96.2 10.5 reduce-scatter.5.cloned.1.call-start
  108.4 14.7 all-to-all-done.2
  140.6 74.5 %all-gather.10.cloned.1.call-done = bf16[2048,6144]{1,0:T(8,128)(2,1)} async-done(((bf16[256,6144]{1,0:T(8,128)(2,1)}), bf16[2048,6144]{1,0:T(8,128)(2,1)}) %all-gather.10.cloned.1.call-update) | async-done | bytes 25165840 | tf_op jit(solution)/shard_map/all_gather | solution.py:181
  215.1 10.0 convolution_add_fusion.3
  230.2 147.6 %all-gather.16.cloned.1.call-done = bf16[8192,2048]{1,0:T(8,128)(2,1)} async-done(((bf16[1024,2048]{1,0:T(8,128)(2,1)}), bf16[8192,2048]{1,0:T(8,128)(2,1)}) %all-gather.16.cloned.1.call-update) | async-done | bytes 33554448 | tf_op jit(solution)/shard_map/all_gather | solution.py:187
  377.8 19.8 fusion.171
  397.6 17.4 fusion.172
  415.0 125.3 %all-gather.14.cloned.1.call-done = bf16[2048,8192]{1,0:T(8,128)(2,1)} async-done(((bf16[256,8192]{1,0:T(8,128)(2,1)}), bf16[2048,8192]{1,0:T(8,128)(2,1)}) %all-gather.14.cloned.1.call-update) | async-done | bytes 33554448 | tf_op jit(solution)/shard_map/all_gather | solution.py:185
  540.4 18.5 convert_reduce_fusion.1
  558.9 18.6 convert_reduce_fusion
  577.5 16.2 convolution_convert_fusion
  609.5 14.5 convolution_add_fusion.2
  668.0 65.2 %collective-permute-done = bf16[128,2048]{1,0:T(8,128)(2,1)S(1)} collective-permute-done((bf16[128,2048]{1,0:T(8,128)(2,1)S(1)}, bf16[128,2048]{1,0:T(8,128)(2,1)S(1)}, u32[]{:S(2)}, u32[]{:S(2)}) %collective-permute-start) | collective-permute-done | bytes 524320 | tf_op jit(solution)/shard_map/ppermute | solution.py:18
  745.8 17.1 collective-permute-done.3
  774.4 54.3 %collective-permute-done.14 = bf16[128,2048]{1,0:T(8,128)(2,1)S(1)} collective-permute-done((bf16[128,2048]{1,0:T(8,128)(2,1)S(1)}, bf16[128,2048]{1,0:T(8,128)(2,1)S(1)}, u32[]{:S(2)}, u32[]{:S(2)}) %collective-permute-start.14) | collective-permute-done | bytes 524320 | tf_op jit(solution)/shard_map/ppermute | solution.py:18
  840.2 16.6 collective-permute-done.17
  880.1 13.6 multiply_reduce_fusion.1
  893.7 13.5 multiply_convert_fusion.1
  915.4 10.4 fusion.167
  970.8 9.1 fusion.169
  981.0 13.7 multiply_reduce_fusion
  994.7 13.9 multiply_convert_fusion
  1020.8 7.8 fusion.63
  1035.5 9.8 fusion.65
  1077.1 20.7 collective-permute-done.48
  1104.7 16.7 collective-permute-done.44
  1124.8 23.6 collective-permute-done.41
  1167.7 25.6 collective-permute-done.55
  1197.2 13.6 collective-permute-done.52
  1212.2 15.1 convolution_convert_fusion.2
  1227.4 15.5 convolution_convert_fusion.1
  1242.9 44.7 %pad_maximum_fusion = bf16[2048,16384]{1,0:T(8,128)(2,1)} fusion(bf16[2048,2048]{1,0:T(8,128)(2,1)} %convolution_convert_fusion.3, bf16[2048,8192]{1,0:T(8,128)(2,1)} %convolution_convert_fusion.1, bf16[2048,6144]{1,0:T(8,128)(2,1)} %convolution_convert_fusion.2), kind=kLoop, calls=%fused_computation.5 | loop fusion | flops 201326592 | bytes 134217728 | tf_op jit(solution)/shard_map/concatenate | solution.py:84
  1291.0 17.5 all-gather.4
  1308.5 9.6 all-gather.3
  1335.8 22.8 fusion.97
  1358.6 18.7 fusion.96
  1377.3 19.1 fusion.61
  1396.4 15.1 fusion.62
  1418.2 17.5 convolution_add_fusion.4
  1435.8 19.7 multiply_reduce_fusion.3
  1462.0 45.2 %all-reduce.22 = (bf16[2048]{0:T(1024)(128)(2,1)S(1)}, bf16[2048]{0:T(1024)(128)(2,1)S(1)}, bf16[6144]{0:T(1024)(128)(2,1)S(1)}, bf16[2048]{0:T(1024)(128)(2,1)S(1)}, bf16[8192]{0:T(1024)(128)(2,1)S(1)}) all-reduce(bf16[2048]{0:T(1024)(128)(2,1)S(1)} %add_convert_fusion.12, ...), channel_id=2, replica_groups=mesh['rep'=4,'shard'=8] {'shard'}, use_global_device_ids=true, to_apply=%region_25.27.clone | all-reduce | flops 20480 | bytes 81920
  1519.2 186.8 %reduce-scatter.3.cloned.1.call-done = bf16[256,16384]{1,0:T(8,128)(2,1)} async-done(((bf16[2048,16384]{1,0:T(8,128)(2,1)}), bf16[256,16384]{1,0:T(8,128)(2,1)}) %reduce-scatter.3.cloned.1.call-update) | async-done | bytes 8388624 | tf_op jit(solution)/shard_map/reduce_scatter | solution.py:83
  1706.0 840.0 %all-reduce.24 = (f32[256]{0:T(256)}, f32[256]{0:T(256)}, f32[256,16384]{1,0:T(8,128)}, f32[768]{0:T(1024)}, f32[256]{0:T(256)S(1)}, /*index=5*/f32[1024]{0:T(1024)}, f32[1024,2048]{1,0:T(8,128)}) all-reduce(f32[256]{0:T(256)S(1)} %dynamic-slice_convert_fusion.4, ...), channel_id=1, replica_groups=mesh['rep'=4,'shard'=8] {'rep'}, use_global_device_ids=true, to_apply=%region_26.28 | all-reduce | flops 6294016 | bytes 37769216 | tf_op jit(solution)/shard_map/psum | solution.py:119
  (586 shorter events, 366.1 us)
Async XLA Ops:
  7.2 118.4 %all-gather.12.cloned.1.call-start = ((), (), s32[]{:S(2)}) async-start(), calls=%async_computation.7 | async-start | bytes 9437184 | tf_op jit(solution)/shard_map/all_gather | solution.py:183
  7.9 207.1 %all-gather.10.cloned.1.call-start = ((), (), s32[]{:S(2)}) async-start(), calls=%async_computation.6 | async-start | bytes 28311552 | tf_op jit(solution)/shard_map/all_gather | solution.py:181
  8.7 369.1 %all-gather.16.cloned.1.call-start = ((), (), s32[]{:S(2)}) async-start(), calls=%async_computation.9 | async-start | bytes 37748736 | tf_op jit(solution)/shard_map/all_gather | solution.py:187
  9.4 530.9 %all-gather.14.cloned.1.call-start = ((), (), s32[]{:S(2)}) async-start(), calls=%async_computation.8 | async-start | bytes 37748736 | tf_op jit(solution)/shard_map/all_gather | solution.py:185
  32.2 60.5 %all-to-all-start = ((bf16[2,8,16,2048]{3,2,0,1:T(8,128)(2,1)}), bf16[2,8,16,2048]{3,2,0,1:T(8,128)(2,1)S(1)}, u32[]{:S(2)}, u32[]{:S(2)}) async-start(bf16[2,8,16,2048]{3,2,0,1:T(8,128)(2,1)} %copy.92), calls=%async_computation | async-start | bytes 2097152 | tf_op jit(solution)/shard_map/all_to_all | solution.py:161
  96.2 1423.0 %reduce-scatter.5.cloned.1.call-start = ((), (), s32[]{:S(2)}) async-start(), calls=%async_computation.11 | async-start | bytes 37748736 | tf_op jit(solution)/shard_map/reduce_scatter | solution.py:96
  593.8 1112.2 %reduce-scatter.3.cloned.1.call-start = ((), (), s32[]{:S(2)}) async-start(), calls=%async_computation.10 | async-start | bytes 75497472 | tf_op jit(solution)/shard_map/reduce_scatter | solution.py:83
  595.0 55.4 %collective-permute-start.11 = (bf16[128,2048]{0,1:T(8,128)(2,1)}, bf16[128,2048]{0,1:T(8,128)(2,1)}, u32[]{:S(2)}, u32[]{:S(2)}) collective-permute-start(bf16[128,2048]{0,1:T(8,128)(2,1)} %bitcast.18), channel_id=1, source_target_pairs={{0,3},{1,4},{2,5},{3,6},{4,7},{8,11},{9,12},{10,13},{11,14},{12,15... | collective-permute-start | bytes 1572872 | tf_op jit(solution)/shard_map/ppermute | solution.py:18
  599.0 48.8 %collective-permute-start.10 = (bf16[128,2048]{0,1:T(8,128)(2,1)}, bf16[128,2048]{0,1:T(8,128)(2,1)}, u32[]{:S(2)}, u32[]{:S(2)}) collective-permute-start(bf16[128,2048]{0,1:T(8,128)(2,1)} %bitcast.18), channel_id=1, source_target_pairs={{0,4},{1,5},{2,6},{3,7},{8,12},{9,13},{10,14},{11,15},{16,20},{17,... | collective-permute-start | bytes 1572872 | tf_op jit(solution)/shard_map/ppermute | solution.py:18
  601.5 38.0 %collective-permute-start.9 = (bf16[128,2048]{0,1:T(8,128)(2,1)}, bf16[128,2048]{0,1:T(8,128)(2,1)}, u32[]{:S(2)}, u32[]{:S(2)}) collective-permute-start(bf16[128,2048]{0,1:T(8,128)(2,1)} %bitcast.18), channel_id=1, source_target_pairs={{0,5},{1,6},{2,7},{8,13},{9,14},{10,15},{16,21},{17,22},{18,23},{2... | collective-permute-start | bytes 1572872 | tf_op jit(solution)/shard_map/ppermute | solution.py:18
  603.6 33.2 %collective-permute-start.8 = (bf16[128,2048]{0,1:T(8,128)(2,1)}, bf16[128,2048]{0,1:T(8,128)(2,1)}, u32[]{:S(2)}, u32[]{:S(2)}) collective-permute-start(bf16[128,2048]{0,1:T(8,128)(2,1)} %bitcast.18), channel_id=1, source_target_pairs={{0,6},{1,7},{8,14},{9,15},{16,22},{17,23},{24,30},{25,31}} | collective-permute-start | bytes 1572872 | tf_op jit(solution)/shard_map/ppermute | solution.py:18
  639.4 128.6 %collective-permute-start.5 = (bf16[128,2048]{1,0:T(8,128)(2,1)S(1)}, bf16[128,2048]{1,0:T(8,128)(2,1)S(1)}, u32[]{:S(2)}, u32[]{:S(2)}) collective-permute-start(bf16[128,2048]{1,0:T(8,128)(2,1)S(1)} %slice.522), channel_id=1, source_target_pairs={{0,2},{1,3},{2,4},{3,5},{4,6},{5,7},{8,10},{9,11},{10,12},{11,13},... | collective-permute-start | bytes 1572872 | tf_op jit(solution)/shard_map/ppermute | solution.py:18
  647.8 118.1 %collective-permute-start.4 = (bf16[128,2048]{1,0:T(8,128)(2,1)S(1)}, bf16[128,2048]{1,0:T(8,128)(2,1)S(1)}, u32[]{:S(2)}, u32[]{:S(2)}) collective-permute-start(bf16[128,2048]{1,0:T(8,128)(2,1)S(1)} %slice.522), channel_id=1, source_target_pairs={{0,3},{1,4},{2,5},{3,6},{4,7},{8,11},{9,12},{10,13},{11,14},{12,15... | collective-permute-start | bytes 1572872 | tf_op jit(solution)/shard_map/ppermute | solution.py:18
  650.4 87.1 %collective-permute-start.2 = (bf16[128,2048]{1,0:T(8,128)(2,1)S(1)}, bf16[128,2048]{1,0:T(8,128)(2,1)S(1)}, u32[]{:S(2)}, u32[]{:S(2)}) collective-permute-start(bf16[128,2048]{1,0:T(8,128)(2,1)S(1)} %slice.522), channel_id=1, source_target_pairs={{0,5},{1,6},{2,7},{8,13},{9,14},{10,15},{16,21},{17,22},{18,23},{2... | collective-permute-start | bytes 1572872 | tf_op jit(solution)/shard_map/ppermute | solution.py:18
  655.3 80.0 %collective-permute-start.1 = (bf16[128,2048]{1,0:T(8,128)(2,1)S(1)}, bf16[128,2048]{1,0:T(8,128)(2,1)S(1)}, u32[]{:S(2)}, u32[]{:S(2)}) collective-permute-start(bf16[128,2048]{1,0:T(8,128)(2,1)S(1)} %slice.522), channel_id=1, source_target_pairs={{0,6},{1,7},{8,14},{9,15},{16,22},{17,23},{24,30},{25,31}} | collective-permute-start | bytes 1572872 | tf_op jit(solution)/shard_map/ppermute | solution.py:18
  656.9 76.3 %collective-permute-start = (bf16[128,2048]{1,0:T(8,128)(2,1)S(1)}, bf16[128,2048]{1,0:T(8,128)(2,1)S(1)}, u32[]{:S(2)}, u32[]{:S(2)}) collective-permute-start(bf16[128,2048]{1,0:T(8,128)(2,1)S(1)} %slice.522), channel_id=1, source_target_pairs={{0,7},{8,15},{16,23},{24,31}} | collective-permute-start | bytes 1572872 | tf_op jit(solution)/shard_map/ppermute | solution.py:18
  735.3 34.8 %collective-permute-start.6 = (bf16[128,2048]{1,0:T(8,128)(2,1)S(1)}, bf16[128,2048]{1,0:T(8,128)(2,1)S(1)}, u32[]{:S(2)}, u32[]{:S(2)}) collective-permute-start(bf16[128,2048]{1,0:T(8,128)(2,1)S(1)} %slice.522), channel_id=1, source_target_pairs={{0,1},{1,2},{2,3},{3,4},{4,5},{5,6},{6,7},{8,9},{9,10},{10,11},{11... | collective-permute-start | bytes 1572872 | tf_op jit(solution)/shard_map/ppermute | solution.py:18
  737.5 135.9 %collective-permute-start.19 = (bf16[128,2048]{1,0:T(8,128)(2,1)S(1)}, bf16[128,2048]{1,0:T(8,128)(2,1)}, u32[]{:S(2)}, u32[]{:S(2)}) collective-permute-start(bf16[128,2048]{1,0:T(8,128)(2,1)S(1)} %slice.521), channel_id=1, source_target_pairs={{0,2},{1,3},{2,4},{3,5},{4,6},{5,7},{8,10},{9,11},{10,12},{11,13},... | collective-permute-start | bytes 1572872 | tf_op jit(solution)/shard_map/ppermute | solution.py:18
  762.9 106.5 %collective-permute-start.18 = (bf16[128,2048]{1,0:T(8,128)(2,1)S(1)}, bf16[128,2048]{1,0:T(8,128)(2,1)}, u32[]{:S(2)}, u32[]{:S(2)}) collective-permute-start(bf16[128,2048]{1,0:T(8,128)(2,1)S(1)} %slice.521), channel_id=1, source_target_pairs={{0,3},{1,4},{2,5},{3,6},{4,7},{8,11},{9,12},{10,13},{11,14},{12,15... | collective-permute-start | bytes 1572872 | tf_op jit(solution)/shard_map/ppermute | solution.py:18
  765.9 68.0 %collective-permute-start.16 = (bf16[128,2048]{1,0:T(8,128)(2,1)S(1)}, bf16[128,2048]{1,0:T(8,128)(2,1)S(1)}, u32[]{:S(2)}, u32[]{:S(2)}) collective-permute-start(bf16[128,2048]{1,0:T(8,128)(2,1)S(1)} %slice.521), channel_id=1, source_target_pairs={{0,5},{1,6},{2,7},{8,13},{9,14},{10,15},{16,21},{17,22},{18,23},{2... | collective-permute-start | bytes 1572872 | tf_op jit(solution)/shard_map/ppermute | solution.py:18
  768.0 62.9 %collective-permute-start.15 = (bf16[128,2048]{1,0:T(8,128)(2,1)S(1)}, bf16[128,2048]{1,0:T(8,128)(2,1)S(1)}, u32[]{:S(2)}, u32[]{:S(2)}) collective-permute-start(bf16[128,2048]{1,0:T(8,128)(2,1)S(1)} %slice.521), channel_id=1, source_target_pairs={{0,6},{1,7},{8,14},{9,15},{16,22},{17,23},{24,30},{25,31}} | collective-permute-start | bytes 1572872 | tf_op jit(solution)/shard_map/ppermute | solution.py:18
  770.2 58.6 %collective-permute-start.14 = (bf16[128,2048]{1,0:T(8,128)(2,1)S(1)}, bf16[128,2048]{1,0:T(8,128)(2,1)S(1)}, u32[]{:S(2)}, u32[]{:S(2)}) collective-permute-start(bf16[128,2048]{1,0:T(8,128)(2,1)S(1)} %slice.521), channel_id=1, source_target_pairs={{0,7},{8,15},{16,23},{24,31}} | collective-permute-start | bytes 1572872 | tf_op jit(solution)/shard_map/ppermute | solution.py:18
  830.9 45.7 %collective-permute-start.20 = (bf16[128,2048]{1,0:T(8,128)(2,1)S(1)}, bf16[128,2048]{1,0:T(8,128)(2,1)}, u32[]{:S(2)}, u32[]{:S(2)}) collective-permute-start(bf16[128,2048]{1,0:T(8,128)(2,1)S(1)} %slice.521), channel_id=1, source_target_pairs={{0,1},{1,2},{2,3},{3,4},{4,5},{5,6},{6,7},{8,9},{9,10},{10,11},{11... | collective-permute-start | bytes 1572872 | tf_op jit(solution)/shard_map/ppermute | solution.py:18
  833.8 117.8 %collective-permute-start.25 = (bf16[128,2048]{0,1:T(8,128)(2,1)}, bf16[128,2048]{0,1:T(8,128)(2,1)S(1)}, u32[]{:S(2)}, u32[]{:S(2)}) collective-permute-start(bf16[128,2048]{0,1:T(8,128)(2,1)} %bitcast.37), channel_id=1, source_target_pairs={{0,3},{1,4},{2,5},{3,6},{4,7},{8,11},{9,12},{10,13},{11,14},{12,15... | collective-permute-start | bytes 1572872 | tf_op jit(solution)/shard_map/ppermute | solution.py:18
  856.8 92.7 %collective-permute-start.24 = (bf16[128,2048]{0,1:T(8,128)(2,1)}, bf16[128,2048]{0,1:T(8,128)(2,1)S(1)}, u32[]{:S(2)}, u32[]{:S(2)}) collective-permute-start(bf16[128,2048]{0,1:T(8,128)(2,1)} %bitcast.37), channel_id=1, source_target_pairs={{0,4},{1,5},{2,6},{3,7},{8,12},{9,13},{10,14},{11,15},{16,20},{17,... | collective-permute-start | bytes 1572872 | tf_op jit(solution)/shard_map/ppermute | solution.py:18
  869.5 76.9 %collective-permute-start.23 = (bf16[128,2048]{0,1:T(8,128)(2,1)}, bf16[128,2048]{0,1:T(8,128)(2,1)}, u32[]{:S(2)}, u32[]{:S(2)}) collective-permute-start(bf16[128,2048]{0,1:T(8,128)(2,1)} %bitcast.37), channel_id=1, source_target_pairs={{0,5},{1,6},{2,7},{8,13},{9,14},{10,15},{16,21},{17,22},{18,23},{2... | collective-permute-start | bytes 1572872 | tf_op jit(solution)/shard_map/ppermute | solution.py:18
  873.5 59.6 %collective-permute-start.22 = (bf16[128,2048]{0,1:T(8,128)(2,1)}, bf16[128,2048]{0,1:T(8,128)(2,1)S(1)}, u32[]{:S(2)}, u32[]{:S(2)}) collective-permute-start(bf16[128,2048]{0,1:T(8,128)(2,1)} %bitcast.37), channel_id=1, source_target_pairs={{0,6},{1,7},{8,14},{9,15},{16,22},{17,23},{24,30},{25,31}} | collective-permute-start | bytes 1572872 | tf_op jit(solution)/shard_map/ppermute | solution.py:18
  876.7 53.5 %collective-permute-start.21 = (bf16[128,2048]{0,1:T(8,128)(2,1)}, bf16[128,2048]{0,1:T(8,128)(2,1)S(1)}, u32[]{:S(2)}, u32[]{:S(2)}) collective-permute-start(bf16[128,2048]{0,1:T(8,128)(2,1)} %bitcast.37), channel_id=1, source_target_pairs={{0,7},{8,15},{16,23},{24,31}} | collective-permute-start | bytes 1572872 | tf_op jit(solution)/shard_map/ppermute | solution.py:18
  946.3 108.2 %collective-permute-start.34 = (bf16[128,2048]{0,1:T(8,128)(2,1)}, bf16[128,2048]{0,1:T(8,128)(2,1)}, u32[]{:S(2)}, u32[]{:S(2)}) collective-permute-start(bf16[128,2048]{0,1:T(8,128)(2,1)} %bitcast.71), channel_id=1, source_target_pairs={{7,0},{15,8},{23,16},{31,24}} | collective-permute-start | bytes 1572872 | tf_op jit(solution)/shard_map/ppermute | solution.py:18
  949.5 106.5 %collective-permute-start.28 = (bf16[128,2048]{0,1:T(8,128)(2,1)}, bf16[128,2048]{0,1:T(8,128)(2,1)}, u32[]{:S(2)}, u32[]{:S(2)}) collective-permute-start(bf16[128,2048]{0,1:T(8,128)(2,1)} %bitcast.65), channel_id=1, source_target_pairs={{1,0},{2,1},{3,2},{4,3},{5,4},{6,5},{7,6},{9,8},{10,9},{11,10},{12... | collective-permute-start | bytes 1572872 | tf_op jit(solution)/shard_map/ppermute | solution.py:18
  951.6 106.6 %collective-permute-start.33 = (bf16[128,2048]{0,1:T(8,128)(2,1)}, bf16[128,2048]{0,1:T(8,128)(2,1)}, u32[]{:S(2)}, u32[]{:S(2)}) collective-permute-start(bf16[128,2048]{0,1:T(8,128)(2,1)} %bitcast.70), channel_id=1, source_target_pairs={{6,0},{7,1},{14,8},{15,9},{22,16},{23,17},{30,24},{31,25}} | collective-permute-start | bytes 1572872 | tf_op jit(solution)/shard_map/ppermute | solution.py:18
  953.7 105.8 %collective-permute-start.32 = (bf16[128,2048]{0,1:T(8,128)(2,1)}, bf16[128,2048]{0,1:T(8,128)(2,1)}, u32[]{:S(2)}, u32[]{:S(2)}) collective-permute-start(bf16[128,2048]{0,1:T(8,128)(2,1)} %bitcast.69), channel_id=1, source_target_pairs={{5,0},{6,1},{7,2},{13,8},{14,9},{15,10},{21,16},{22,17},{23,18},{2... | collective-permute-start | bytes 1572872 | tf_op jit(solution)/shard_map/ppermute | solution.py:18
  956.9 104.0 %collective-permute-start.31 = (bf16[128,2048]{0,1:T(8,128)(2,1)}, bf16[128,2048]{0,1:T(8,128)(2,1)}, u32[]{:S(2)}, u32[]{:S(2)}) collective-permute-start(bf16[128,2048]{0,1:T(8,128)(2,1)} %bitcast.68), channel_id=1, source_target_pairs={{4,0},{5,1},{6,2},{7,3},{12,8},{13,9},{14,10},{15,11},{20,16},{21,... | collective-permute-start | bytes 1572872 | tf_op jit(solution)/shard_map/ppermute | solution.py:18
  1058.3 39.5 %collective-permute-start.48 = (bf16[128,2048]{0,1:T(8,128)(2,1)S(1)}, bf16[128,2048]{0,1:T(8,128)(2,1)S(1)}, u32[]{:S(2)}, u32[]{:S(2)}) collective-permute-start(bf16[128,2048]{0,1:T(8,128)(2,1)S(1)} %bitcast.361), channel_id=1, source_target_pairs={{7,0},{15,8},{23,16},{31,24}} | collective-permute-start | bytes 1572872 | tf_op jit(solution)/shard_map/ppermute | solution.py:18
  1059.6 39.5 %collective-permute-start.42 = (bf16[128,2048]{0,1:T(8,128)(2,1)S(1)}, bf16[128,2048]{0,1:T(8,128)(2,1)S(1)}, u32[]{:S(2)}, u32[]{:S(2)}) collective-permute-start(bf16[128,2048]{0,1:T(8,128)(2,1)S(1)} %bitcast.360), channel_id=1, source_target_pairs={{1,0},{2,1},{3,2},{4,3},{5,4},{6,5},{7,6},{9,8},{10,9},{11,10},{12... | collective-permute-start | bytes 1572872 | tf_op jit(solution)/shard_map/ppermute | solution.py:18
  1060.9 39.9 %collective-permute-start.47 = (bf16[128,2048]{0,1:T(8,128)(2,1)S(1)}, bf16[128,2048]{0,1:T(8,128)(2,1)S(1)}, u32[]{:S(2)}, u32[]{:S(2)}) collective-permute-start(bf16[128,2048]{0,1:T(8,128)(2,1)S(1)} %bitcast.359), channel_id=1, source_target_pairs={{6,0},{7,1},{14,8},{15,9},{22,16},{23,17},{30,24},{31,25}} | collective-permute-start | bytes 1572872 | tf_op jit(solution)/shard_map/ppermute | solution.py:18
  1068.1 33.9 %collective-permute-start.46 = (bf16[128,2048]{0,1:T(8,128)(2,1)S(1)}, bf16[128,2048]{0,1:T(8,128)(2,1)S(1)}, u32[]{:S(2)}, u32[]{:S(2)}) collective-permute-start(bf16[128,2048]{0,1:T(8,128)(2,1)S(1)} %bitcast.358), channel_id=1, source_target_pairs={{5,0},{6,1},{7,2},{13,8},{14,9},{15,10},{21,16},{22,17},{23,18},{2... | collective-permute-start | bytes 1572872 | tf_op jit(solution)/shard_map/ppermute | solution.py:18
  1100.8 47.6 %collective-permute-start.41 = (bf16[128,2048]{0,1:T(8,128)(2,1)S(1)}, bf16[128,2048]{0,1:T(8,128)(2,1)S(1)}, u32[]{:S(2)}, u32[]{:S(2)}) collective-permute-start(bf16[128,2048]{0,1:T(8,128)(2,1)S(1)} %bitcast.354), channel_id=1, source_target_pairs={{7,0},{15,8},{23,16},{31,24}} | collective-permute-start | bytes 1572872 | tf_op jit(solution)/shard_map/ppermute | solution.py:18
  1102.1 47.5 %collective-permute-start.35 = (bf16[128,2048]{0,1:T(8,128)(2,1)S(1)}, bf16[128,2048]{0,1:T(8,128)(2,1)S(1)}, u32[]{:S(2)}, u32[]{:S(2)}) collective-permute-start(bf16[128,2048]{0,1:T(8,128)(2,1)S(1)} %bitcast.353), channel_id=1, source_target_pairs={{1,0},{2,1},{3,2},{4,3},{5,4},{6,5},{7,6},{9,8},{10,9},{11,10},{12... | collective-permute-start | bytes 1572872 | tf_op jit(solution)/shard_map/ppermute | solution.py:18
  1103.4 48.8 %collective-permute-start.40 = (bf16[128,2048]{0,1:T(8,128)(2,1)S(1)}, bf16[128,2048]{0,1:T(8,128)(2,1)S(1)}, u32[]{:S(2)}, u32[]{:S(2)}) collective-permute-start(bf16[128,2048]{0,1:T(8,128)(2,1)S(1)} %bitcast.351), channel_id=1, source_target_pairs={{6,0},{7,1},{14,8},{15,9},{22,16},{23,17},{30,24},{31,25}} | collective-permute-start | bytes 1572872 | tf_op jit(solution)/shard_map/ppermute | solution.py:18
  1122.7 37.2 %collective-permute-start.38 = (bf16[128,2048]{0,1:T(8,128)(2,1)S(1)}, bf16[128,2048]{0,1:T(8,128)(2,1)S(1)}, u32[]{:S(2)}, u32[]{:S(2)}) collective-permute-start(bf16[128,2048]{0,1:T(8,128)(2,1)S(1)} %bitcast.348), channel_id=1, source_target_pairs={{4,0},{5,1},{6,2},{7,3},{12,8},{13,9},{14,10},{15,11},{20,16},{21,... | collective-permute-start | bytes 1572872 | tf_op jit(solution)/shard_map/ppermute | solution.py:18
  1152.2 41.1 %collective-permute-start.55 = (bf16[128,2048]{0,1:T(8,128)(2,1)S(1)}, bf16[128,2048]{0,1:T(8,128)(2,1)S(1)}, u32[]{:S(2)}, u32[]{:S(2)}) collective-permute-start(bf16[128,2048]{0,1:T(8,128)(2,1)S(1)} %bitcast.345), channel_id=1, source_target_pairs={{7,0},{15,8},{23,16},{31,24}} | collective-permute-start | bytes 1572872 | tf_op jit(solution)/shard_map/ppermute | solution.py:18
  1153.5 41.1 %collective-permute-start.49 = (bf16[128,2048]{0,1:T(8,128)(2,1)S(1)}, bf16[128,2048]{0,1:T(8,128)(2,1)S(1)}, u32[]{:S(2)}, u32[]{:S(2)}) collective-permute-start(bf16[128,2048]{0,1:T(8,128)(2,1)S(1)} %bitcast.344), channel_id=1, source_target_pairs={{1,0},{2,1},{3,2},{4,3},{5,4},{6,5},{7,6},{9,8},{10,9},{11,10},{12... | collective-permute-start | bytes 1572872 | tf_op jit(solution)/shard_map/ppermute | solution.py:18
  1159.9 37.3 %collective-permute-start.54 = (bf16[128,2048]{0,1:T(8,128)(2,1)S(1)}, bf16[128,2048]{0,1:T(8,128)(2,1)S(1)}, u32[]{:S(2)}, u32[]{:S(2)}) collective-permute-start(bf16[128,2048]{0,1:T(8,128)(2,1)S(1)} %bitcast.343), channel_id=1, source_target_pairs={{6,0},{7,1},{14,8},{15,9},{22,16},{23,17},{30,24},{31,25}} | collective-permute-start | bytes 1572872 | tf_op jit(solution)/shard_map/ppermute | solution.py:18
  1162.5 34.7 %collective-permute-start.53 = (bf16[128,2048]{0,1:T(8,128)(2,1)S(1)}, bf16[128,2048]{0,1:T(8,128)(2,1)S(1)}, u32[]{:S(2)}, u32[]{:S(2)}) collective-permute-start(bf16[128,2048]{0,1:T(8,128)(2,1)S(1)} %bitcast.342), channel_id=1, source_target_pairs={{5,0},{6,1},{7,2},{13,8},{14,9},{15,10},{21,16},{22,17},{23,18},{2... | collective-permute-start | bytes 1572872 | tf_op jit(solution)/shard_map/ppermute | solution.py:18
  1166.4 44.4 %collective-permute-start.52 = (bf16[128,2048]{0,1:T(8,128)(2,1)S(1)}, bf16[128,2048]{0,1:T(8,128)(2,1)S(1)}, u32[]{:S(2)}, u32[]{:S(2)}) collective-permute-start(bf16[128,2048]{0,1:T(8,128)(2,1)S(1)} %bitcast.341), channel_id=1, source_target_pairs={{4,0},{5,1},{6,2},{7,3},{12,8},{13,9},{14,10},{15,11},{20,16},{21,... | collective-permute-start | bytes 1572872 | tf_op jit(solution)/shard_map/ppermute | solution.py:18
  1413.9 44.1 %all-to-all-start.1 = ((bf16[2,8,16,2048]{3,2,0,1:T(8,128)(2,1)}), bf16[2,8,16,2048]{3,2,0,1:T(8,128)(2,1)}, u32[]{:S(2)}, u32[]{:S(2)}) async-start(bf16[2,8,16,2048]{3,2,0,1:T(8,128)(2,1)} %pad_maximum_fusion.3), calls=%async_computation.1 | async-start | bytes 2097152 | tf_op jit(solution)/shard_map/all_to_all | solution.py:338
  1458.0 55.2 %all-to-all-start.3 = ((bf16[2,8,16,2048]{3,2,0,1:T(8,128)(2,1)}), bf16[2,8,16,2048]{3,2,0,1:T(8,128)(2,1)S(1)}, u32[]{:S(2)}, u32[]{:S(2)}) async-start(bf16[2,8,16,2048]{3,2,0,1:T(8,128)(2,1)} %pad_maximum_fusion.4), calls=%async_computation.3 | async-start | bytes 2097152 | tf_op jit(solution)/shard_map/all_to_all | solution.py:339
  (150 other events, 6437.1 us)
Sparse Core Ops, SparseCore 0:
  9.9 66.3 all-gather.11
  78.2 136.8 all-gather.9
  217.0 160.7 all-gather.15
  379.5 160.7 all-gather.13
  593.9 311.7 reduce-scatter.4
  1287.9 418.0 reduce-scatter.2
where the time goes:
time: 2580 us; the launch traced here: 2570 us
  blocking collectives  963 us (37%)
  waiting for transfers between devices  826 us (32%)
  matrix products  385 us (15%)
  local copies, waits for them, and re-layouts  135 us (5%)
  starting transfers between devices  134 us (5%)
  other arithmetic  106 us (4%)
    psum x1, blocking collectives, reduce_grads(): lax.psum((wide, deep, scattered[0], scattered[1], scattered[2], scattered...  840 us
    ppermute x56, waiting for transfers between devices, shifted(): return lax.ppermute(block, axis, route)  275 us
    reduce_scatter x1, waiting for transfers between devices, reduce_grads(): lax.psum_scatter(jnp.concatenate([contract_first(hn_rows, dqkv_rows), con...  187 us
    all_gather x1, waiting for transfers between devices, body(): lax.all_gather(shards[8], 'shard', axis=0, tiled=True)  148 us
    dot_general x8, matrix products, contract_last(): lax.dot_general(left, right, (((1,), (1,)), ((), ())), preferred_element_...  129 us
    all_gather x1, waiting for transfers between devices, body(): lax.all_gather(shards[6], 'shard', axis=0, tiled=True)  125 us
    ppermute x56, starting transfers between devices, shifted(): return lax.ppermute(block, axis, route)  106 us
    all_gather x1, waiting for transfers between devices, body(): lax.all_gather(shards[2], 'shard', axis=0, tiled=True)  74.5 us
  transfers between devices with their start and end apart: 66, of which 22 were waited for; matrix products, arithmetic and copies ran while one was open for 21% of the time, Pallas kernels for 0%

commit v1 on v0

--- a/solution.py
+++ b/solution.py
@@ -10,6 +10,27 @@
 BLOCK = 128
 MICRO = 2
 MAXBLK = 8
+
+
+def stops_all_fix(raw):
+    shaped = lax.axis_size("shard")
+    even, carry_out, reply = (shaped, lax.axis_index("shard"), raw.shape[0])
+    copies = tuple((j * even if b == 0 else j for b, j in enumerate(raw.shape)))
+    odd = lax.dynamic_update_slice_in_dim(
+        jnp.zeros(copies, raw.dtype), raw, carry_out * reply, axis=0
+    )
+    z_new = block_out = raw
+    for t in range(1, even // 2 + 1):
+        z_new = lax.ppermute(z_new, "shard", tuple(((b, (b + 1) % even) for b in range(even))))
+        odd = lax.dynamic_update_slice_in_dim(odd, z_new, (carry_out - t) % even * reply, axis=0)
+        if 2 * t < even:
+            block_out = lax.ppermute(
+                block_out, "shard", tuple(((b, (b - 1) % even) for b in range(even)))
+            )
+            odd = lax.dynamic_update_slice_in_dim(
+                odd, block_out, (carry_out + t) % even * reply, axis=0
+            )
+    return odd
 
 
 def shifted(block, axis, distance):
@@ -182,7 +203,7 @@
         lax.all_gather(shards[3], "shard", axis=0, tiled=True),
         lax.all_gather(shards[4], "shard", axis=0, tiled=True),
         lax.all_gather(shards[5], "shard", axis=0, tiled=True),
-        lax.all_gather(shards[6], "shard", axis=0, tiled=True),
+        stops_all_fix(shards[6]),
         lax.all_gather(shards[7], "shard", axis=0, tiled=True),
         lax.all_gather(shards[8], "shard", axis=0, tiled=True),
         lax.all_gather(shards[9], "shard", axis=0, tiled=True),

time: 2580 us -> 2720 us (1.054)
  blocking collectives: 963 us -> 1110 us
  waiting for transfers between devices: 826 us -> 777 us
  local copies, waits for them, and re-layouts: 135 us -> 179 us
    ppermute x0 -> x7, waiting for transfers between devices: none -> 294 us  [the longest x4 292 us: stops_all_fix(): lax.ppermute(z_new, 'shard', tuple(((b, (b + 1) % even) for b in range(ev...]
    all_gather x1, blocking collectives: 24.7 us -> 177 us  [body(): lax.all_gather(shards[1], 'shard', axis=0, tiled=True)]
    all_gather x1, waiting for transfers between devices: 148 us -> 0.02 us  [body(): lax.all_gather(shards[8], 'shard', axis=0, tiled=True)]
    all_gather x1 -> x0, waiting for transfers between devices: 125 us -> none  [body(): lax.all_gather(shards[6], 'shard', axis=0, tiled=True)]
    all_gather x1, waiting for transfers between devices: 74.5 us -> 0.01 us  [body(): lax.all_gather(shards[2], 'shard', axis=0, tiled=True)]
    dynamic_update_slice x0 -> x8, local copies, waits for them, and re-layouts: none -> 32.7 us  [the longest x4 18.9 us: stops_all_fix(): lax.dynamic_update_slice_in_dim(odd, z_new, (carry_out - t) % even * repl...]
  transfers between devices with their start and end apart: 66 -> 72, of which waited for: 22 -> 23; matrix products, arithmetic and copies ran while one was open for 21% -> 20% of each run, Pallas kernels for 0% -> 0%
where the time goes in v1:
time: 2720 us; the launch traced here: 2710 us
  blocking collectives  1110 us (41%)
  waiting for transfers between devices  777 us (29%)
  matrix products  378 us (14%)
  local copies, waits for them, and re-layouts  179 us (7%)
  starting transfers between devices  132 us (5%)
  other arithmetic  107 us (4%)
    psum x1, blocking collectives, reduce_grads(): lax.psum((wide, deep, scattered[0], scattered[1], scattered[2], scattered...  839 us
    ppermute x4, waiting for transfers between devices, stops_all_fix(): lax.ppermute(z_new, 'shard', tuple(((b, (b + 1) % even) for b in range(ev...  292 us
    ppermute x56, waiting for transfers between devices, shifted(): return lax.ppermute(block, axis, route)  269 us
    reduce_scatter x1, waiting for transfers between devices, reduce_grads(): lax.psum_scatter(jnp.concatenate([contract_first(hn_rows, dqkv_rows), con...  192 us
    all_gather x1, blocking collectives, body(): lax.all_gather(shards[1], 'shard', axis=0, tiled=True)  177 us
    dot_general x8, matrix products, contract_last(): lax.dot_general(left, right, (((1,), (1,)), ((), ())), preferred_element_...  127 us
    ppermute x56, starting transfers between devices, shifted(): return lax.ppermute(block, axis, route)  105 us
  transfers between devices with their start and end apart: 72, of which 23 were waited for; matrix products, arithmetic and copies ran while one was open for 20% of the time, Pallas kernels for 0%

profile of v1, /device:TPU:0, one launch (start us, length us, event | category | flops | bytes accessed | tf_op | source)
XLA Modules:
  0.0 2706.9 jit_solution(17629179283110796931)
XLA Ops:
  13.5 11.4 scatter_fusion
  39.6 114.9 %collective-permute-done.14 = bf16[256,8192]{1,0:T(8,128)(2,1)} collective-permute-done((bf16[256,8192]{1,0:T(8,128)(2,1)}, bf16[256,8192]{1,0:T(8,128)(2,1)}, u32[]{:S(2)}, u32[]{:S(2)}) %collective-permute-start.14) | collective-permute-done | bytes 4194336 | tf_op jit(solution)/shard_map/ppermute | solution.py:24
  165.7 176.9 %all-gather.1 = bf16[8,1,256]{2,1,0:T(2,128)(2,1)S(1)} all-gather(bf16[1,1,256]{2,1,0:T(2,128)(2,1)S(1)} %reshape.784), channel_id=1, replica_groups=mesh['rep'=4,'shard'=8] {'shard'}, dimensions={0}, use_global_device_ids=true | all-gather | bytes 4608 | tf_op jit(solution)/shard_map/all_gather | solution.py:201
  342.7 8.9 all-gather
  351.7 7.9 all_gather.33
  359.6 9.6 all-gather.2
  370.2 11.7 broadcast_in_dim.237
  389.8 19.8 all-to-all-done.2
  421.7 159.2 %collective-permute-done.18 = bf16[256,8192]{1,0:T(8,128)(2,1)} collective-permute-done((bf16[256,8192]{1,0:T(8,128)(2,1)}, bf16[256,8192]{1,0:T(8,128)(2,1)}, u32[]{:S(2)}, u32[]{:S(2)}) %collective-permute-start.18) | collective-permute-done | bytes 4194336 | tf_op jit(solution)/shard_map/ppermute | solution.py:24
  611.7 18.3 collective-permute-done.20
  634.6 10.2 convolution_add_fusion.3
  649.5 17.4 fusion.171
  667.0 18.5 convert_reduce_fusion.1
  685.5 17.4 fusion.172
  702.9 18.7 convert_reduce_fusion
  721.6 16.1 convolution_convert_fusion
  752.4 14.5 convolution_add_fusion.2
  810.0 65.2 %collective-permute-done = bf16[128,2048]{1,0:T(8,128)(2,1)S(1)} collective-permute-done((bf16[128,2048]{1,0:T(8,128)(2,1)S(1)}, bf16[128,2048]{1,0:T(8,128)(2,1)S(1)}, u32[]{:S(2)}, u32[]{:S(2)}) %collective-permute-start) | collective-permute-done | bytes 524320 | tf_op jit(solution)/shard_map/ppermute | solution.py:39
  887.8 17.4 collective-permute-done.3
  916.6 56.5 %collective-permute-done.21 = bf16[128,2048]{1,0:T(8,128)(2,1)S(1)} collective-permute-done((bf16[128,2048]{1,0:T(8,128)(2,1)S(1)}, bf16[128,2048]{1,0:T(8,128)(2,1)S(1)}, u32[]{:S(2)}, u32[]{:S(2)}) %collective-permute-start.21) | collective-permute-done | bytes 524320 | tf_op jit(solution)/shard_map/ppermute | solution.py:39
  984.6 8.8 collective-permute-done.24
  1017.9 13.8 multiply_reduce_fusion.1
  1031.7 13.6 multiply_convert_fusion.1
  1053.5 10.4 fusion.167
  1109.6 9.1 fusion.169
  1119.8 13.7 multiply_reduce_fusion
  1133.5 13.9 multiply_convert_fusion
  1159.7 7.8 fusion.63
  1174.4 9.8 fusion.65
  1215.8 20.8 collective-permute-done.55
  1243.5 16.6 collective-permute-done.51
  1263.5 23.6 collective-permute-done.48
  1306.4 25.6 collective-permute-done.62
  1335.9 13.6 collective-permute-done.59
  1350.9 15.1 convolution_convert_fusion.2
  1366.1 15.6 convolution_convert_fusion.1
  1381.6 44.7 %pad_maximum_fusion = bf16[2048,16384]{1,0:T(8,128)(2,1)} fusion(bf16[2048,2048]{1,0:T(8,128)(2,1)} %convolution_convert_fusion.3, bf16[2048,8192]{1,0:T(8,128)(2,1)} %convolution_convert_fusion.1, bf16[2048,6144]{1,0:T(8,128)(2,1)} %convolution_convert_fusion.2), kind=kLoop, calls=%fused_computation.5 | loop fusion | flops 201326592 | bytes 134217728 | tf_op jit(solution)/shard_map/concatenate | solution.py:105
  1429.8 17.5 all-gather.4
  1447.3 9.6 all-gather.3
  1476.2 19.0 fusion.97
  1495.2 18.5 fusion.96
  1513.8 22.3 convolution_add_fusion.4
  1536.1 20.1 multiply_reduce_fusion.3
  1563.1 14.5 fusion.62
  1577.7 13.9 fusion.61
  1596.8 45.2 %all-reduce.22 = (bf16[2048]{0:T(1024)(128)(2,1)S(1)}, bf16[2048]{0:T(1024)(128)(2,1)S(1)}, bf16[6144]{0:T(1024)(128)(2,1)S(1)}, bf16[2048]{0:T(1024)(128)(2,1)S(1)}, bf16[8192]{0:T(1024)(128)(2,1)S(1)}) all-reduce(bf16[2048]{0:T(1024)(128)(2,1)S(1)} %add_convert_fusion.12, ...), channel_id=2, replica_groups=mesh['rep'=4,'shard'=8] {'shard'}, use_global_device_ids=true, to_apply=%region_25.27.clone | all-reduce | flops 20480 | bytes 81920
  1654.0 192.0 %reduce-scatter.3.cloned.1.call-done = bf16[256,16384]{1,0:T(8,128)(2,1)} async-done(((bf16[2048,16384]{1,0:T(8,128)(2,1)}), bf16[256,16384]{1,0:T(8,128)(2,1)}) %reduce-scatter.3.cloned.1.call-update) | async-done | bytes 8388624 | tf_op jit(solution)/shard_map/reduce_scatter | solution.py:104
  1846.0 839.4 %all-reduce.24 = (f32[256]{0:T(256)}, f32[256]{0:T(256)}, f32[256,16384]{1,0:T(8,128)}, f32[768]{0:T(1024)}, f32[256]{0:T(256)S(1)}, /*index=5*/f32[1024]{0:T(1024)}, f32[1024,2048]{1,0:T(8,128)}) all-reduce(f32[256]{0:T(256)S(1)} %dynamic-slice_convert_fusion.4, ...), channel_id=1, replica_groups=mesh['rep'=4,'shard'=8] {'rep'}, use_global_device_ids=true, to_apply=%region_26.28 | all-reduce | flops 6294016 | bytes 37769216 | tf_op jit(solution)/shard_map/psum | solution.py:140
  (604 shorter events, 409.0 us)
Async XLA Ops:
  7.2 589.9 %all-gather.11.cloned.1.call-start = ((), (), s32[]{:S(2)}) async-start(), calls=%async_computation.7 | async-start | bytes 9437184 | tf_op jit(solution)/shard_map/all_gather | solution.py:204
  7.9 626.7 %all-gather.9.cloned.1.call-start = ((), (), s32[]{:S(2)}) async-start(), calls=%async_computation.6 | async-start | bytes 28311552 | tf_op jit(solution)/shard_map/all_gather | solution.py:202
  8.7 640.8 %all-gather.13.cloned.1.call-start = ((), (), s32[]{:S(2)}) async-start(), calls=%async_computation.8 | async-start | bytes 37748736 | tf_op jit(solution)/shard_map/all_gather | solution.py:208
  9.4 145.0 %collective-permute-start.14 = (bf16[256,8192]{1,0:T(8,128)(2,1)}, bf16[256,8192]{1,0:T(8,128)(2,1)}, u32[]{:S(2)}, u32[]{:S(2)}) collective-permute-start(bf16[256,8192]{1,0:T(8,128)(2,1)} %param.26), channel_id=1, source_target_pairs={{0,1},{1,2},{2,3},{3,4},{4,5},{5,6},{6,7},{7,0},{8,9},{9,10},{10,1... | collective-permute-start | bytes 12582920 | tf_op jit(solution)/shard_map/ppermute | solution.py:24
  9.9 152.7 %collective-permute-start.15 = (bf16[256,8192]{1,0:T(8,128)(2,1)}, bf16[256,8192]{1,0:T(8,128)(2,1)}, u32[]{:S(2)}, u32[]{:S(2)}) collective-permute-start(bf16[256,8192]{1,0:T(8,128)(2,1)} %param.26), channel_id=1, source_target_pairs={{0,7},{1,0},{2,1},{3,2},{4,3},{5,4},{6,5},{7,6},{8,15},{9,8},{10,9... | collective-permute-start | bytes 12582920 | tf_op jit(solution)/shard_map/ppermute | solution.py:27
  35.5 348.7 %all-to-all-start = ((bf16[2,8,16,2048]{3,2,0,1:T(8,128)(2,1)}), bf16[2,8,16,2048]{3,2,0,1:T(8,128)(2,1)S(1)}, u32[]{:S(2)}, u32[]{:S(2)}) async-start(bf16[2,8,16,2048]{3,2,0,1:T(8,128)(2,1)} %copy.92), calls=%async_computation | async-start | bytes 2097152 | tf_op jit(solution)/shard_map/all_to_all | solution.py:182
  154.4 234.0 %collective-permute-start.16 = (bf16[256,8192]{1,0:T(8,128)(2,1)}, bf16[256,8192]{1,0:T(8,128)(2,1)}, u32[]{:S(2)}, u32[]{:S(2)}) collective-permute-start(bf16[256,8192]{1,0:T(8,128)(2,1)} %collective-permute-done.14), channel_id=1, source_target_pairs={{0,1},{1,2},{2,3},{3,4},{4,5},{5,6},{6,7},{7,0},{8,9},{9,10},{10,1... | collective-permute-start | bytes 12582920 | tf_op jit(solution)/shard_map/ppermute | solution.py:24
  162.6 249.4 %collective-permute-start.17 = (bf16[256,8192]{1,0:T(8,128)(2,1)}, bf16[256,8192]{1,0:T(8,128)(2,1)}, u32[]{:S(2)}, u32[]{:S(2)}) collective-permute-start(bf16[256,8192]{1,0:T(8,128)(2,1)} %collective-permute-done.15), channel_id=1, source_target_pairs={{0,7},{1,0},{2,1},{3,2},{4,3},{5,4},{6,5},{7,6},{8,15},{9,8},{10,9... | collective-permute-start | bytes 12582920 | tf_op jit(solution)/shard_map/ppermute | solution.py:27
  387.7 1266.2 %reduce-scatter.5.cloned.1.call-start = ((), (), s32[]{:S(2)}) async-start(), calls=%async_computation.10 | async-start | bytes 37748736 | tf_op jit(solution)/shard_map/reduce_scatter | solution.py:117
  388.4 192.5 %collective-permute-start.18 = (bf16[256,8192]{1,0:T(8,128)(2,1)}, bf16[256,8192]{1,0:T(8,128)(2,1)}, u32[]{:S(2)}, u32[]{:S(2)}) collective-permute-start(bf16[256,8192]{1,0:T(8,128)(2,1)} %collective-permute-done.16), channel_id=1, source_target_pairs={{0,1},{1,2},{2,3},{3,4},{4,5},{5,6},{6,7},{7,0},{8,9},{9,10},{10,1... | collective-permute-start | bytes 12582920 | tf_op jit(solution)/shard_map/ppermute | solution.py:24
  412.0 182.9 %collective-permute-start.19 = (bf16[256,8192]{1,0:T(8,128)(2,1)}, bf16[256,8192]{1,0:T(8,128)(2,1)S(1)}, u32[]{:S(2)}, u32[]{:S(2)}) collective-permute-start(bf16[256,8192]{1,0:T(8,128)(2,1)} %collective-permute-done.17), channel_id=1, source_target_pairs={{0,7},{1,0},{2,1},{3,2},{4,3},{5,4},{6,5},{7,6},{8,15},{9,8},{10,9... | collective-permute-start | bytes 12582920 | tf_op jit(solution)/shard_map/ppermute | solution.py:27
  580.9 49.1 %collective-permute-start.20 = (bf16[256,8192]{1,0:T(8,128)(2,1)}, bf16[256,8192]{1,0:T(8,128)(2,1)}, u32[]{:S(2)}, u32[]{:S(2)}) collective-permute-start(bf16[256,8192]{1,0:T(8,128)(2,1)} %collective-permute-done.18), channel_id=1, source_target_pairs={{0,1},{1,2},{2,3},{3,4},{4,5},{5,6},{6,7},{7,0},{8,9},{9,10},{10,1... | collective-permute-start | bytes 12582920 | tf_op jit(solution)/shard_map/ppermute | solution.py:24
  737.7 1108.2 %reduce-scatter.3.cloned.1.call-start = ((), (), s32[]{:S(2)}) async-start(), calls=%async_computation.9 | async-start | bytes 75497472 | tf_op jit(solution)/shard_map/reduce_scatter | solution.py:104
  738.9 53.4 %collective-permute-start.11 = (bf16[128,2048]{0,1:T(8,128)(2,1)}, bf16[128,2048]{0,1:T(8,128)(2,1)}, u32[]{:S(2)}, u32[]{:S(2)}) collective-permute-start(bf16[128,2048]{0,1:T(8,128)(2,1)} %bitcast.18), channel_id=1, source_target_pairs={{0,3},{1,4},{2,5},{3,6},{4,7},{8,11},{9,12},{10,13},{11,14},{12,15... | collective-permute-start | bytes 1572872 | tf_op jit(solution)/shard_map/ppermute | solution.py:39
  741.0 48.7 %collective-permute-start.10 = (bf16[128,2048]{0,1:T(8,128)(2,1)}, bf16[128,2048]{0,1:T(8,128)(2,1)}, u32[]{:S(2)}, u32[]{:S(2)}) collective-permute-start(bf16[128,2048]{0,1:T(8,128)(2,1)} %bitcast.18), channel_id=1, source_target_pairs={{0,4},{1,5},{2,6},{3,7},{8,12},{9,13},{10,14},{11,15},{16,20},{17,... | collective-permute-start | bytes 1572872 | tf_op jit(solution)/shard_map/ppermute | solution.py:39
  744.3 38.4 %collective-permute-start.9 = (bf16[128,2048]{0,1:T(8,128)(2,1)}, bf16[128,2048]{0,1:T(8,128)(2,1)}, u32[]{:S(2)}, u32[]{:S(2)}) collective-permute-start(bf16[128,2048]{0,1:T(8,128)(2,1)} %bitcast.18), channel_id=1, source_target_pairs={{0,5},{1,6},{2,7},{8,13},{9,14},{10,15},{16,21},{17,22},{18,23},{2... | collective-permute-start | bytes 1572872 | tf_op jit(solution)/shard_map/ppermute | solution.py:39
  782.7 127.5 %collective-permute-start.5 = (bf16[128,2048]{1,0:T(8,128)(2,1)S(1)}, bf16[128,2048]{1,0:T(8,128)(2,1)S(1)}, u32[]{:S(2)}, u32[]{:S(2)}) collective-permute-start(bf16[128,2048]{1,0:T(8,128)(2,1)S(1)} %slice.522), channel_id=1, source_target_pairs={{0,2},{1,3},{2,4},{3,5},{4,6},{5,7},{8,10},{9,11},{10,12},{11,13},... | collective-permute-start | bytes 1572872 | tf_op jit(solution)/shard_map/ppermute | solution.py:39
  789.8 118.3 %collective-permute-start.4 = (bf16[128,2048]{1,0:T(8,128)(2,1)S(1)}, bf16[128,2048]{1,0:T(8,128)(2,1)S(1)}, u32[]{:S(2)}, u32[]{:S(2)}) collective-permute-start(bf16[128,2048]{1,0:T(8,128)(2,1)S(1)} %slice.522), channel_id=1, source_target_pairs={{0,3},{1,4},{2,5},{3,6},{4,7},{8,11},{9,12},{10,13},{11,14},{12,15... | collective-permute-start | bytes 1572872 | tf_op jit(solution)/shard_map/ppermute | solution.py:39
  792.3 87.2 %collective-permute-start.2 = (bf16[128,2048]{1,0:T(8,128)(2,1)S(1)}, bf16[128,2048]{1,0:T(8,128)(2,1)S(1)}, u32[]{:S(2)}, u32[]{:S(2)}) collective-permute-start(bf16[128,2048]{1,0:T(8,128)(2,1)S(1)} %slice.522), channel_id=1, source_target_pairs={{0,5},{1,6},{2,7},{8,13},{9,14},{10,15},{16,21},{17,22},{18,23},{2... | collective-permute-start | bytes 1572872 | tf_op jit(solution)/shard_map/ppermute | solution.py:39
  797.3 80.1 %collective-permute-start.1 = (bf16[128,2048]{1,0:T(8,128)(2,1)S(1)}, bf16[128,2048]{1,0:T(8,128)(2,1)S(1)}, u32[]{:S(2)}, u32[]{:S(2)}) collective-permute-start(bf16[128,2048]{1,0:T(8,128)(2,1)S(1)} %slice.522), channel_id=1, source_target_pairs={{0,6},{1,7},{8,14},{9,15},{16,22},{17,23},{24,30},{25,31}} | collective-permute-start | bytes 1572872 | tf_op jit(solution)/shard_map/ppermute | solution.py:39
  798.8 76.4 %collective-permute-start = (bf16[128,2048]{1,0:T(8,128)(2,1)S(1)}, bf16[128,2048]{1,0:T(8,128)(2,1)S(1)}, u32[]{:S(2)}, u32[]{:S(2)}) collective-permute-start(bf16[128,2048]{1,0:T(8,128)(2,1)S(1)} %slice.522), channel_id=1, source_target_pairs={{0,7},{8,15},{16,23},{24,31}} | collective-permute-start | bytes 1572872 | tf_op jit(solution)/shard_map/ppermute | solution.py:39
  879.5 130.4 %collective-permute-start.26 = (bf16[128,2048]{1,0:T(8,128)(2,1)S(1)}, bf16[128,2048]{1,0:T(8,128)(2,1)}, u32[]{:S(2)}, u32[]{:S(2)}) collective-permute-start(bf16[128,2048]{1,0:T(8,128)(2,1)S(1)} %slice.521), channel_id=1, source_target_pairs={{0,2},{1,3},{2,4},{3,5},{4,6},{5,7},{8,10},{9,11},{10,12},{11,13},... | collective-permute-start | bytes 1572872 | tf_op jit(solution)/shard_map/ppermute | solution.py:39
  905.2 100.8 %collective-permute-start.25 = (bf16[128,2048]{1,0:T(8,128)(2,1)S(1)}, bf16[128,2048]{1,0:T(8,128)(2,1)}, u32[]{:S(2)}, u32[]{:S(2)}) collective-permute-start(bf16[128,2048]{1,0:T(8,128)(2,1)S(1)} %slice.521), channel_id=1, source_target_pairs={{0,3},{1,4},{2,5},{3,6},{4,7},{8,11},{9,12},{10,13},{11,14},{12,15... | collective-permute-start | bytes 1572872 | tf_op jit(solution)/shard_map/ppermute | solution.py:39
  908.1 70.2 %collective-permute-start.23 = (bf16[128,2048]{1,0:T(8,128)(2,1)S(1)}, bf16[128,2048]{1,0:T(8,128)(2,1)S(1)}, u32[]{:S(2)}, u32[]{:S(2)}) collective-permute-start(bf16[128,2048]{1,0:T(8,128)(2,1)S(1)} %slice.521), channel_id=1, source_target_pairs={{0,5},{1,6},{2,7},{8,13},{9,14},{10,15},{16,21},{17,22},{18,23},{2... | collective-permute-start | bytes 1572872 | tf_op jit(solution)/shard_map/ppermute | solution.py:39
  910.2 65.1 %collective-permute-start.22 = (bf16[128,2048]{1,0:T(8,128)(2,1)S(1)}, bf16[128,2048]{1,0:T(8,128)(2,1)S(1)}, u32[]{:S(2)}, u32[]{:S(2)}) collective-permute-start(bf16[128,2048]{1,0:T(8,128)(2,1)S(1)} %slice.521), channel_id=1, source_target_pairs={{0,6},{1,7},{8,14},{9,15},{16,22},{17,23},{24,30},{25,31}} | collective-permute-start | bytes 1572872 | tf_op jit(solution)/shard_map/ppermute | solution.py:39
  912.4 60.8 %collective-permute-start.21 = (bf16[128,2048]{1,0:T(8,128)(2,1)S(1)}, bf16[128,2048]{1,0:T(8,128)(2,1)S(1)}, u32[]{:S(2)}, u32[]{:S(2)}) collective-permute-start(bf16[128,2048]{1,0:T(8,128)(2,1)S(1)} %slice.521), channel_id=1, source_target_pairs={{0,7},{8,15},{16,23},{24,31}} | collective-permute-start | bytes 1572872 | tf_op jit(solution)/shard_map/ppermute | solution.py:39
  975.3 37.9 %collective-permute-start.27 = (bf16[128,2048]{1,0:T(8,128)(2,1)S(1)}, bf16[128,2048]{1,0:T(8,128)(2,1)}, u32[]{:S(2)}, u32[]{:S(2)}) collective-permute-start(bf16[128,2048]{1,0:T(8,128)(2,1)S(1)} %slice.521), channel_id=1, source_target_pairs={{0,1},{1,2},{2,3},{3,4},{4,5},{5,6},{6,7},{8,9},{9,10},{10,11},{11... | collective-permute-start | bytes 1572872 | tf_op jit(solution)/shard_map/ppermute | solution.py:39
  978.3 112.2 %collective-permute-start.32 = (bf16[128,2048]{0,1:T(8,128)(2,1)}, bf16[128,2048]{0,1:T(8,128)(2,1)S(1)}, u32[]{:S(2)}, u32[]{:S(2)}) collective-permute-start(bf16[128,2048]{0,1:T(8,128)(2,1)} %bitcast.37), channel_id=1, source_target_pairs={{0,3},{1,4},{2,5},{3,6},{4,7},{8,11},{9,12},{10,13},{11,14},{12,15... | collective-permute-start | bytes 1572872 | tf_op jit(solution)/shard_map/ppermute | solution.py:39
  993.4 94.9 %collective-permute-start.31 = (bf16[128,2048]{0,1:T(8,128)(2,1)}, bf16[128,2048]{0,1:T(8,128)(2,1)S(1)}, u32[]{:S(2)}, u32[]{:S(2)}) collective-permute-start(bf16[128,2048]{0,1:T(8,128)(2,1)} %bitcast.37), channel_id=1, source_target_pairs={{0,4},{1,5},{2,6},{3,7},{8,12},{9,13},{10,14},{11,15},{16,20},{17,... | collective-permute-start | bytes 1572872 | tf_op jit(solution)/shard_map/ppermute | solution.py:39
  1006.0 79.2 %collective-permute-start.30 = (bf16[128,2048]{0,1:T(8,128)(2,1)}, bf16[128,2048]{0,1:T(8,128)(2,1)}, u32[]{:S(2)}, u32[]{:S(2)}) collective-permute-start(bf16[128,2048]{0,1:T(8,128)(2,1)} %bitcast.37), channel_id=1, source_target_pairs={{0,5},{1,6},{2,7},{8,13},{9,14},{10,15},{16,21},{17,22},{18,23},{2... | collective-permute-start | bytes 1572872 | tf_op jit(solution)/shard_map/ppermute | solution.py:39
  1010.0 61.9 %collective-permute-start.29 = (bf16[128,2048]{0,1:T(8,128)(2,1)}, bf16[128,2048]{0,1:T(8,128)(2,1)S(1)}, u32[]{:S(2)}, u32[]{:S(2)}) collective-permute-start(bf16[128,2048]{0,1:T(8,128)(2,1)} %bitcast.37), channel_id=1, source_target_pairs={{0,6},{1,7},{8,14},{9,15},{16,22},{17,23},{24,30},{25,31}} | collective-permute-start | bytes 1572872 | tf_op jit(solution)/shard_map/ppermute | solution.py:39
  1013.2 55.1 %collective-permute-start.28 = (bf16[128,2048]{0,1:T(8,128)(2,1)}, bf16[128,2048]{0,1:T(8,128)(2,1)S(1)}, u32[]{:S(2)}, u32[]{:S(2)}) collective-permute-start(bf16[128,2048]{0,1:T(8,128)(2,1)} %bitcast.37), channel_id=1, source_target_pairs={{0,7},{8,15},{16,23},{24,31}} | collective-permute-start | bytes 1572872 | tf_op jit(solution)/shard_map/ppermute | solution.py:39
  1085.2 108.2 %collective-permute-start.41 = (bf16[128,2048]{0,1:T(8,128)(2,1)}, bf16[128,2048]{0,1:T(8,128)(2,1)}, u32[]{:S(2)}, u32[]{:S(2)}) collective-permute-start(bf16[128,2048]{0,1:T(8,128)(2,1)} %bitcast.71), channel_id=1, source_target_pairs={{7,0},{15,8},{23,16},{31,24}} | collective-permute-start | bytes 1572872 | tf_op jit(solution)/shard_map/ppermute | solution.py:39
  1088.3 106.5 %collective-permute-start.35 = (bf16[128,2048]{0,1:T(8,128)(2,1)}, bf16[128,2048]{0,1:T(8,128)(2,1)}, u32[]{:S(2)}, u32[]{:S(2)}) collective-permute-start(bf16[128,2048]{0,1:T(8,128)(2,1)} %bitcast.65), channel_id=1, source_target_pairs={{1,0},{2,1},{3,2},{4,3},{5,4},{6,5},{7,6},{9,8},{10,9},{11,10},{12... | collective-permute-start | bytes 1572872 | tf_op jit(solution)/shard_map/ppermute | solution.py:39
  1090.4 106.7 %collective-permute-start.40 = (bf16[128,2048]{0,1:T(8,128)(2,1)}, bf16[128,2048]{0,1:T(8,128)(2,1)}, u32[]{:S(2)}, u32[]{:S(2)}) collective-permute-start(bf16[128,2048]{0,1:T(8,128)(2,1)} %bitcast.70), channel_id=1, source_target_pairs={{6,0},{7,1},{14,8},{15,9},{22,16},{23,17},{30,24},{31,25}} | collective-permute-start | bytes 1572872 | tf_op jit(solution)/shard_map/ppermute | solution.py:39
  1092.6 105.9 %collective-permute-start.39 = (bf16[128,2048]{0,1:T(8,128)(2,1)}, bf16[128,2048]{0,1:T(8,128)(2,1)}, u32[]{:S(2)}, u32[]{:S(2)}) collective-permute-start(bf16[128,2048]{0,1:T(8,128)(2,1)} %bitcast.69), channel_id=1, source_target_pairs={{5,0},{6,1},{7,2},{13,8},{14,9},{15,10},{21,16},{22,17},{23,18},{2... | collective-permute-start | bytes 1572872 | tf_op jit(solution)/shard_map/ppermute | solution.py:39
  1095.7 104.0 %collective-permute-start.38 = (bf16[128,2048]{0,1:T(8,128)(2,1)}, bf16[128,2048]{0,1:T(8,128)(2,1)}, u32[]{:S(2)}, u32[]{:S(2)}) collective-permute-start(bf16[128,2048]{0,1:T(8,128)(2,1)} %bitcast.68), channel_id=1, source_target_pairs={{4,0},{5,1},{6,2},{7,3},{12,8},{13,9},{14,10},{15,11},{20,16},{21,... | collective-permute-start | bytes 1572872 | tf_op jit(solution)/shard_map/ppermute | solution.py:39
  1197.1 39.5 %collective-permute-start.55 = (bf16[128,2048]{0,1:T(8,128)(2,1)S(1)}, bf16[128,2048]{0,1:T(8,128)(2,1)S(1)}, u32[]{:S(2)}, u32[]{:S(2)}) collective-permute-start(bf16[128,2048]{0,1:T(8,128)(2,1)S(1)} %bitcast.361), channel_id=1, source_target_pairs={{7,0},{15,8},{23,16},{31,24}} | collective-permute-start | bytes 1572872 | tf_op jit(solution)/shard_map/ppermute | solution.py:39
  1198.5 39.5 %collective-permute-start.49 = (bf16[128,2048]{0,1:T(8,128)(2,1)S(1)}, bf16[128,2048]{0,1:T(8,128)(2,1)S(1)}, u32[]{:S(2)}, u32[]{:S(2)}) collective-permute-start(bf16[128,2048]{0,1:T(8,128)(2,1)S(1)} %bitcast.360), channel_id=1, source_target_pairs={{1,0},{2,1},{3,2},{4,3},{5,4},{6,5},{7,6},{9,8},{10,9},{11,10},{12... | collective-permute-start | bytes 1572872 | tf_op jit(solution)/shard_map/ppermute | solution.py:39
  1199.8 39.9 %collective-permute-start.54 = (bf16[128,2048]{0,1:T(8,128)(2,1)S(1)}, bf16[128,2048]{0,1:T(8,128)(2,1)S(1)}, u32[]{:S(2)}, u32[]{:S(2)}) collective-permute-start(bf16[128,2048]{0,1:T(8,128)(2,1)S(1)} %bitcast.359), channel_id=1, source_target_pairs={{6,0},{7,1},{14,8},{15,9},{22,16},{23,17},{30,24},{31,25}} | collective-permute-start | bytes 1572872 | tf_op jit(solution)/shard_map/ppermute | solution.py:39
  1239.6 47.4 %collective-permute-start.48 = (bf16[128,2048]{0,1:T(8,128)(2,1)S(1)}, bf16[128,2048]{0,1:T(8,128)(2,1)S(1)}, u32[]{:S(2)}, u32[]{:S(2)}) collective-permute-start(bf16[128,2048]{0,1:T(8,128)(2,1)S(1)} %bitcast.354), channel_id=1, source_target_pairs={{7,0},{15,8},{23,16},{31,24}} | collective-permute-start | bytes 1572872 | tf_op jit(solution)/shard_map/ppermute | solution.py:39
  1240.9 47.4 %collective-permute-start.42 = (bf16[128,2048]{0,1:T(8,128)(2,1)S(1)}, bf16[128,2048]{0,1:T(8,128)(2,1)S(1)}, u32[]{:S(2)}, u32[]{:S(2)}) collective-permute-start(bf16[128,2048]{0,1:T(8,128)(2,1)S(1)} %bitcast.353), channel_id=1, source_target_pairs={{1,0},{2,1},{3,2},{4,3},{5,4},{6,5},{7,6},{9,8},{10,9},{11,10},{12... | collective-permute-start | bytes 1572872 | tf_op jit(solution)/shard_map/ppermute | solution.py:39
  1242.2 48.7 %collective-permute-start.47 = (bf16[128,2048]{0,1:T(8,128)(2,1)S(1)}, bf16[128,2048]{0,1:T(8,128)(2,1)S(1)}, u32[]{:S(2)}, u32[]{:S(2)}) collective-permute-start(bf16[128,2048]{0,1:T(8,128)(2,1)S(1)} %bitcast.351), channel_id=1, source_target_pairs={{6,0},{7,1},{14,8},{15,9},{22,16},{23,17},{30,24},{31,25}} | collective-permute-start | bytes 1572872 | tf_op jit(solution)/shard_map/ppermute | solution.py:39
  1290.9 41.1 %collective-permute-start.62 = (bf16[128,2048]{0,1:T(8,128)(2,1)S(1)}, bf16[128,2048]{0,1:T(8,128)(2,1)S(1)}, u32[]{:S(2)}, u32[]{:S(2)}) collective-permute-start(bf16[128,2048]{0,1:T(8,128)(2,1)S(1)} %bitcast.345), channel_id=1, source_target_pairs={{7,0},{15,8},{23,16},{31,24}} | collective-permute-start | bytes 1572872 | tf_op jit(solution)/shard_map/ppermute | solution.py:39
  1292.2 41.1 %collective-permute-start.56 = (bf16[128,2048]{0,1:T(8,128)(2,1)S(1)}, bf16[128,2048]{0,1:T(8,128)(2,1)S(1)}, u32[]{:S(2)}, u32[]{:S(2)}) collective-permute-start(bf16[128,2048]{0,1:T(8,128)(2,1)S(1)} %bitcast.344), channel_id=1, source_target_pairs={{1,0},{2,1},{3,2},{4,3},{5,4},{6,5},{7,6},{9,8},{10,9},{11,10},{12... | collective-permute-start | bytes 1572872 | tf_op jit(solution)/shard_map/ppermute | solution.py:39
  1298.6 37.3 %collective-permute-start.61 = (bf16[128,2048]{0,1:T(8,128)(2,1)S(1)}, bf16[128,2048]{0,1:T(8,128)(2,1)S(1)}, u32[]{:S(2)}, u32[]{:S(2)}) collective-permute-start(bf16[128,2048]{0,1:T(8,128)(2,1)S(1)} %bitcast.343), channel_id=1, source_target_pairs={{6,0},{7,1},{14,8},{15,9},{22,16},{23,17},{30,24},{31,25}} | collective-permute-start | bytes 1572872 | tf_op jit(solution)/shard_map/ppermute | solution.py:39
  1305.1 44.4 %collective-permute-start.59 = (bf16[128,2048]{0,1:T(8,128)(2,1)S(1)}, bf16[128,2048]{0,1:T(8,128)(2,1)S(1)}, u32[]{:S(2)}, u32[]{:S(2)}) collective-permute-start(bf16[128,2048]{0,1:T(8,128)(2,1)S(1)} %bitcast.341), channel_id=1, source_target_pairs={{4,0},{5,1},{6,2},{7,3},{12,8},{13,9},{14,10},{15,11},{20,16},{21,... | collective-permute-start | bytes 1572872 | tf_op jit(solution)/shard_map/ppermute | solution.py:39
  1592.7 55.3 %all-to-all-start.1 = ((bf16[2,8,16,2048]{3,2,0,1:T(8,128)(2,1)}), bf16[2,8,16,2048]{3,2,0,1:T(8,128)(2,1)S(1)}, u32[]{:S(2)}, u32[]{:S(2)}) async-start(bf16[2,8,16,2048]{3,2,0,1:T(8,128)(2,1)} %pad_maximum_fusion.3), calls=%async_computation.1 | async-start | bytes 2097152 | tf_op jit(solution)/shard_map/all_to_all | solution.py:359
  (155 other events, 7147.6 us)
Sparse Core Ops, SparseCore 0:
  9.9 90.1 all-gather.10
  102.0 225.1 all-gather.8
  329.1 248.0 all-gather.12
  737.8 314.1 reduce-scatter.4
  1426.6 419.2 reduce-scatter.2
